TPU v7x, 32 devices: a whole 2x2x4 slice. The times are simulated.
32 devices in a mesh: region: 8 (over y, x, core), tm: 4 (over z).
Axes of the slice: x: 2, y: 2, z: 4, core: 2. Of those that a mesh axis runs over, the one named last changes fastest.
Arguments:
- jacobian: bfloat16 [24576, 2048], P(('region', 'tm')), may hold values from -0.375 to 0.375
- foot_block: int32 [24576], P(('region', 'tm')), may hold values from 0 to 63, as said below
- foot_time: int32 [24576], P(('region', 'tm')), may hold values from 0 to 208, as said below
- obs_weight: bfloat16 [24576], P(('region', 'tm')), may hold values from 0.29882812 to 3
- misfit: bfloat16 [24576], P(('region', 'tm')), may hold values from -6 to 6
- kept_list: int32 [16384], P(('region', 'tm')), may hold values from 0 to 767, as said below
- kept_count: int32 [32], P(('region', 'tm')), may hold values from 256 to 512, as said below
- prior_std: float32 [224, 64, 128], P('tm', 'region'), may hold values from 0.4 to 11
- time_factor: float32 [224, 224], replicated, may hold values from -0.3 to 1.3
Outputs:
- solution: float32 [224, 64, 128], P('tm', 'region')
- residual: float32 [224, 64, 128], P('tm', 'region')
Inputs may be any that keep to these rules, and one draw needn't show every extreme that they name: `kept_list`: the 512 entries of one device are distinct row numbers within that device's own 768 rows. A device keeps the rows named by the first kept_count entries of its list. Region block of the footprint; the block is owned by the region index foot_block // 8. A footprint covers steps foot_time to foot_time + 15, all in the time window foot_time // 56: foot_time % 56 <= 40. Among the kept rows of one device, at most 24 have footprints owned by any one device (region index foot_block // 8, time index foot_time // 56); in every draw some owning device gets exactly 24 kept rows from every device.
All inputs are finite; a program needn't handle non-finite values.
Results may differ from a plain program's by a relative error of at most 0.0004.
Values may be sent and summed in bfloat16 or wider, within the bound.
No kernel may reach another device: no remote copies, remote signals or barrier semaphores. Data moves between devices by JAX's collectives and lax.ppermute only.
A program may use at most 128 MiB of HBM per device.

v0:
```python
import jax
import jax.numpy as jnp
from jax import lax
from jax.sharding import PartitionSpec as P

ITERS = 2


def conjugate(rhs, operator, inner):
    solution = jnp.zeros_like(rhs)
    residual = rhs
    direction = rhs
    norm_now = inner(residual, residual)
    for iteration in range(ITERS):
        image = operator(direction)
        alpha = norm_now / inner(direction, image)
        solution = solution + alpha * direction
        residual = residual - alpha * image
        norm_next = inner(residual, residual)
        direction = residual + norm_next / norm_now * direction
        norm_now = norm_next
    return (solution, residual)


def local(
    jacobian,
    foot_block,
    foot_time,
    obs_weight,
    misfit,
    kept_list,
    kept_count,
    prior_std,
    time_factor,
):
    time_dev, reg_dev, cell_count = prior_std.shape
    region_count = lax.axis_size("region")
    window_count = lax.axis_size("tm")
    devices = region_count * window_count
    keep_rows = kept_list.shape[0]
    lag_cells = jacobian.shape[1]
    lag_steps = lag_cells // cell_count
    capacity = 3 * keep_rows // (2 * devices)
    total_slots = devices * capacity
    own_start = lax.axis_index("tm") * time_dev
    chosen = jacobian[kept_list]
    blocks = foot_block[kept_list]
    starts = foot_time[kept_list]
    is_kept = jnp.arange(keep_rows, dtype=jnp.int32) < kept_count[0]
    target = blocks // reg_dev * window_count + starts // time_dev
    onehot = (
        (target[:, None] == jnp.arange(devices, dtype=jnp.int32)[None, :]) & is_kept[:, None]
    ).astype(jnp.int32)
    slot_rank = jnp.sum(jnp.cumsum(onehot, axis=0) * onehot, axis=1) - 1
    position = jnp.where(is_kept, target * capacity + slot_rank, total_slots)
    placing = jnp.stack([blocks % reg_dev, starts % time_dev], axis=1)
    labels = jnp.stack([obs_weight[kept_list], misfit[kept_list]], axis=1)
    rows_out = (
        jnp.zeros((total_slots, lag_cells), jnp.bfloat16).at[position].set(chosen, mode="drop")
    )
    place_out = jnp.zeros((total_slots, 2), jnp.int32).at[position].set(placing, mode="drop")
    label_out = jnp.zeros((total_slots, 2), jnp.bfloat16).at[position].set(labels, mode="drop")
    rows_in, place_in, label_in = (
        lax.all_to_all(rows_out, ("region", "tm"), split_axis=0, concat_axis=0, tiled=True),
        lax.all_to_all(place_out, ("region", "tm"), split_axis=0, concat_axis=0, tiled=True),
        lax.all_to_all(label_out, ("region", "tm"), split_axis=0, concat_axis=0, tiled=True),
    )
    shaped = rows_in.reshape(total_slots, lag_steps, cell_count)
    index = (
        place_in[:, 1:2] + jnp.arange(lag_steps, dtype=jnp.int32)[None, :]
    ) * reg_dev + place_in[:, 0:1]
    weight_in = label_in[:, 0].astype(jnp.float32)
    misfit_in = label_in[:, 1].astype(jnp.float32)

    def observe(field):
        slab = field.reshape(time_dev * reg_dev, cell_count)[index]
        return jnp.sum(shaped.astype(jnp.float32) * slab, axis=(1, 2))

    def spread(values):
        terms = shaped.astype(jnp.float32) * values[:, None, None]
        flat = jnp.zeros((time_dev * reg_dev, cell_count), jnp.float32).at[index].add(terms)
        return flat.reshape(time_dev, reg_dev, cell_count)

    def sounding_term(field):
        return spread(weight_in * observe(field))

    source_term = spread(weight_in * misfit_in)

    def narrow(field):
        piece = lax.all_gather(field, "tm", axis=0, tiled=True)
        block = lax.dynamic_slice(time_factor, (own_start, 0), (time_dev, piece.shape[0]))
        total = jnp.dot(
            block,
            piece.reshape(piece.shape[0], reg_dev * cell_count),
            precision=lax.Precision.HIGHEST,
        )
        return prior_std * total.reshape(time_dev, reg_dev, cell_count)

    def widen(values):
        scaled = (prior_std * values).reshape(time_dev, reg_dev * cell_count)
        block = lax.dynamic_slice(
            time_factor, (own_start, 0), (time_dev, lax.axis_size("tm") * time_dev)
        )
        total = lax.psum_scatter(
            jnp.dot(block.T, scaled, precision=lax.Precision.HIGHEST),
            "tm",
            scatter_dimension=0,
            tiled=True,
        )
        return total.reshape(time_dev, reg_dev, cell_count)

    def inner(first, second):
        return lax.psum(jnp.sum(first * second), ("region", "tm"))

    def operator(field):
        return field + widen(sounding_term(narrow(field)))

    return conjugate(widen(source_term), operator, inner)


def solution(mesh):
    return jax.shard_map(
        local,
        mesh=mesh,
        in_specs=(
            P(("region", "tm"), None),
            P(("region", "tm")),
            P(("region", "tm")),
            P(("region", "tm")),
            P(("region", "tm")),
            P(("region", "tm")),
            P(("region", "tm")),
            P("tm", "region", None),
            P(),
        ),
        out_specs=(P("tm", "region", None), P("tm", "region", None)),
        check_vma=False,
    )
```

profile of v0, /device:TPU:0, one launch (start us, length us, event | category | flops | bytes accessed | tf_op | source)
XLA Modules:
  0.0 717.6 jit_solution(6456427700297044240)
XLA Ops:
  8.8 3.7 gather_fusion.3
  12.5 3.7 gather_fusion.2
  16.2 3.4 gather_fusion
  19.6 3.4 gather_fusion.1
  23.0 1.2 reduce-window.6
  24.8 1.8 scatter_custom_fusion.2
  26.7 0.9 copy.38
  27.5 7.3 %all-to-all-start.2 = ((bf16[32,24,2]{1,2,0:T(2,128)(2,1)}), bf16[32,24,2]{1,2,0:T(2,128)(2,1)S(1)}, u32[]{:S(2)}, u32[]{:S(2)}) async-start(bf16[32,24,2]{1,2,0:T(2,128)(2,1)} %copy.38), calls=%async_computation.2 | async-start | bytes 32768 | tf_op jit(solution)/shard_map/all_to_all | solution.py:66
  34.9 0.8 copy.32
  35.7 2.2 scatter_custom_fusion
  37.9 0.9 copy.34
  38.8 3.2 all-to-all-done.2
  42.0 2.8 all-to-all-start
  44.8 12.4 %scatter_custom_fusion.1 = bf16[768,2048]{1,0:T(8,128)(2,1)} fusion(s32[512]{0:T(512)} %bitcast.176, bf16[768,2048]{1,0:T(8,128)(2,1)S(1)} %copy-done, s32[1024]{0:T(1024)} %copy-done.14, bf16[]{:T(256)} %constant.73.clone.1), kind=kCustom, calls=%fused_computation.18 | custom fusion | bytes 3146240 | tf_op jit(solution)/shard_map/scatter | solution.py:59
  57.3 5.9 all-to-all-start.1
  64.9 68.4 %all-to-all-done.1 = bf16[32,24,2048]{2,1,0:T(8,128)(2,1)S(1)} async-done(((bf16[32,24,2048]{2,1,0:T(8,128)(2,1)}), bf16[32,24,2048]{2,1,0:T(8,128)(2,1)S(1)}, u32[]{:S(2)}, u32[]{:S(2)}) %all-to-all-start.1) | async-done | bytes 3145760 | tf_op jit(solution)/shard_map/all_to_all | solution.py:64
  133.2 1.0 copy.53
  134.2 4.4 bitcast_multiply_fusion.2
  138.8 66.0 %scatter_custom_fusion.3 = f32[448,128]{1,0:T(8,128)S(1)} fusion(s32[12288]{0:T(1024)S(1)} %copy-done.13, f32[12288,128]{1,0:T(8,128)} %bitcast.157, f32[]{:T(128)} %constant.62.clone.1), kind=kCustom, calls=%fused_computation.64 | custom fusion | flops 1572864 | bytes 229888 | tf_op jit(solution)/shard_map/scatter-add | solution.py:81
  204.8 2.7 fusion.18
  207.6 25.6 %reduce-scatter.4.cloned.1.call-done = f32[56,1024]{1,0:T(8,128)} async-done(((f32[224,1024]{1,0:T(8,128)}), f32[56,1024]{1,0:T(8,128)}) %reduce-scatter.4.cloned.1.call-update) | async-done | bytes 229392 | tf_op jit(solution)/shard_map/reduce_scatter | solution.py:104
  233.2 1.0 copy.55
  234.2 18.9 %all_gather.6 = f32[224,8,128]{2,1,0:T(8,128)S(1)} all-gather(f32[56,8,128]{2,1,0:T(8,128)S(1)} %bitcast.162), channel_id=1, replica_groups=mesh['region'=8,'tm'=4] {'tm'}, dimensions={0}, use_global_device_ids=true | all-gather | bytes 1146880 | tf_op jit(solution)/shard_map/all_gather | solution.py:90
  253.1 1.6 convolution_multiply_fusion.1
  254.8 41.0 %gather_fusion.4 = f32[12288,128]{1,0:T(8,128)} fusion(f32[448,128]{1,0:T(8,128)S(1)} %bitcast.153, s32[12288]{0:T(1024)S(1)} %broadcast_clamp_fusion), kind=kCustom, calls=%fused_computation.5 | custom fusion | bytes 12632064 | tf_op jit(solution)/shard_map/gather | solution.py:76
  295.8 7.3 %gather.37 = f32[32,24,2048]{2,1,0:T(8,128)} reshape(f32[12288,128]{1,0:T(8,128)} %gather_fusion.4) | data formatting | bytes 12582912 | tf_op jit(solution)/shard_map/gather | solution.py:76
  303.1 3.5 multiply_reduce_fusion.1
  306.7 5.7 bitcast_multiply_fusion.1
  312.5 66.0 %scatter_custom_fusion.4 = f32[448,128]{1,0:T(8,128)S(1)} fusion(s32[12288]{0:T(1024)S(1)} %copy-done.13, f32[12288,128]{1,0:T(8,128)} %bitcast.158, f32[]{:T(128)} %constant.62.clone.1), kind=kCustom, calls=%fused_computation.62 | custom fusion | flops 1572864 | bytes 229888 | tf_op jit(solution)/shard_map/scatter-add | solution.py:81
  378.6 1.9 fusion.15
  380.5 25.3 %reduce-scatter.6.cloned.1.call-done = f32[56,1024]{1,0:T(8,128)} async-done(((f32[224,1024]{1,0:T(8,128)}), f32[56,1024]{1,0:T(8,128)}) %reduce-scatter.6.cloned.1.call-update) | async-done | bytes 229392 | tf_op jit(solution)/shard_map/reduce_scatter | solution.py:104
  405.8 1.6 multiply_reduce_fusion.3
  407.4 38.9 %all-reduce = (f32[]{:T(128)}, f32[]{:T(128)}) all-reduce(f32[]{:T(128)} %get-tuple-element.3, f32[]{:T(128)} %get-tuple-element.2), channel_id=1, replica_groups=mesh['region'=8,'tm'=4] {'region','tm'}, use_global_device_ids=true, to_apply=%region_9.10 | all-reduce | flops 2 | bytes 16 | tf_op jit(solution)/shard_map/psum | solution.py:113
  448.2 1.0 copy.58
  449.2 41.2 %psum.30 = f32[]{:T(128)} all-reduce(f32[]{:T(128)} %multiply_reduce_fusion.2), channel_id=1, replica_groups=mesh['region'=8,'tm'=4] {'region','tm'}, use_global_device_ids=true, to_apply=%region_16.17 | all-reduce | flops 1 | bytes 8 | tf_op jit(solution)/shard_map/psum | solution.py:113
  491.7 19.1 %all_gather.7 = f32[224,8,128]{2,1,0:T(8,128)S(1)} all-gather(f32[56,8,128]{2,1,0:T(8,128)S(1)} %multiply_add_fusion.1), channel_id=1, replica_groups=mesh['region'=8,'tm'=4] {'tm'}, dimensions={0}, use_global_device_ids=true | all-gather | bytes 1146880 | tf_op jit(solution)/shard_map/all_gather | solution.py:90
  511.6 41.0 %gather_fusion.5 = f32[12288,128]{1,0:T(8,128)} fusion(f32[448,128]{1,0:T(8,128)S(1)} %bitcast.152, s32[12288]{0:T(1024)S(1)} %broadcast_clamp_fusion), kind=kCustom, calls=%fused_computation.6 | custom fusion | bytes 12632064 | tf_op jit(solution)/shard_map/gather | solution.py:76
  552.7 7.2 %gather.39 = f32[32,24,2048]{2,1,0:T(8,128)} reshape(f32[12288,128]{1,0:T(8,128)} %gather_fusion.5) | data formatting | bytes 12582912 | tf_op jit(solution)/shard_map/gather | solution.py:76
  559.9 3.5 multiply_reduce_fusion
  563.5 5.8 bitcast_multiply_fusion
  569.3 66.6 %scatter_custom_fusion.5 = f32[448,128]{1,0:T(8,128)} fusion(s32[12288]{0:T(1024)S(1)} %copy-done.13, f32[12288,128]{1,0:T(8,128)} %bitcast.156, f32[]{:T(128)} %constant.62.clone.1), kind=kCustom, calls=%fused_computation.60 | custom fusion | flops 1572864 | bytes 229888 | tf_op jit(solution)/shard_map/scatter-add | solution.py:81
  635.9 1.0 bitcast_multiply_fusion.3
  636.9 2.7 fusion.10
  639.6 26.1 %reduce-scatter.8.cloned.1.call-done = f32[56,1024]{1,0:T(8,128)} async-done(((f32[224,1024]{1,0:T(8,128)}), f32[56,1024]{1,0:T(8,128)}) %reduce-scatter.8.cloned.1.call-update) | async-done | bytes 229392 | tf_op jit(solution)/shard_map/reduce_scatter | solution.py:104
  665.7 1.8 fusion.7
  667.6 38.8 %psum.31 = f32[]{:T(128)} all-reduce(f32[]{:T(128)} %fusion.7), channel_id=1, replica_groups=mesh['region'=8,'tm'=4] {'region','tm'}, use_global_device_ids=true, to_apply=%region_21.22 | all-reduce | flops 1 | bytes 8 | tf_op jit(solution)/shard_map/psum | solution.py:113
  707.7 1.0 copy.61
  708.7 1.9 fusion.9
  (78 shorter events, 5.2 us)
Async XLA Ops:
  7.2 37.7 %copy-start = (bf16[768,2048]{1,0:T(8,128)(2,1)S(1)}, bf16[768,2048]{1,0:T(8,128)(2,1)}, u32[]{:S(2)}) copy-start(bf16[768,2048]{1,0:T(8,128)(2,1)} %param.9) | copy-start | bytes 9437188
  8.8 14.2 %copy-start.14 = (s32[1024]{0:T(1024)}, s32[1024]{0:T(1024)S(1)}, u32[]{:S(2)}) copy-start(s32[1024]{0:T(1024)S(1)} %pad_clamp_fusion) | copy-start | bytes 12292
  24.8 10.1 %copy-start.15 = (s32[512,1]{0,1:T(1,128)}, s32[512,1]{0,1:T(1,128)S(1)}, u32[]{:S(2)}) copy-start(s32[512,1]{0,1:T(1,128)S(1)} %get-tuple-element.17) | copy-start | bytes 6148
  27.5 14.5 %all-to-all-start.2 = ((bf16[32,24,2]{1,2,0:T(2,128)(2,1)}), bf16[32,24,2]{1,2,0:T(2,128)(2,1)S(1)}, u32[]{:S(2)}, u32[]{:S(2)}) async-start(bf16[32,24,2]{1,2,0:T(2,128)(2,1)} %copy.38), calls=%async_computation.2 | async-start | bytes 32768 | tf_op jit(solution)/shard_map/all_to_all | solution.py:66
  42.0 15.3 %all-to-all-start = ((s32[32,24,2]{1,2,0:T(2,128)}), s32[32,24,2]{1,2,0:T(2,128)S(1)}, u32[]{:S(2)}, u32[]{:S(2)}) async-start(s32[32,24,2]{1,2,0:T(2,128)} %copy.34), calls=%async_computation | async-start | bytes 65536 | tf_op jit(solution)/shard_map/all_to_all | solution.py:65
  57.3 75.9 %all-to-all-start.1 = ((bf16[32,24,2048]{2,1,0:T(8,128)(2,1)}), bf16[32,24,2048]{2,1,0:T(8,128)(2,1)S(1)}, u32[]{:S(2)}, u32[]{:S(2)}) async-start(bf16[32,24,2048]{2,1,0:T(8,128)(2,1)} %bitcast.155), calls=%async_computation.1 | async-start | bytes 6291456 | tf_op jit(solution)/shard_map/all_to_all | solution.py:64
  63.2 169.9 %reduce-scatter.4.cloned.1.call-start = ((), (), s32[]{:S(2)}) async-start(), calls=%async_computation.6 | async-start | bytes 1146880 | tf_op jit(solution)/shard_map/reduce_scatter | solution.py:104
  133.2 5.4 copy-start.3
  134.2 4.6 copy-start.2
  134.2 4.6 copy-start.13
  134.2 70.6 %copy-start.6 = (f32[56,8,128]{2,1,0:T(8,128)S(1)}, f32[56,8,128]{2,1,0:T(8,128)}, u32[]{:S(2)}) copy-start(f32[56,8,128]{2,1,0:T(8,128)} %param.16) | copy-start | bytes 688132
  207.6 198.2 %reduce-scatter.6.cloned.1.call-start = ((), (), s32[]{:S(2)}) async-start(), calls=%async_computation.7 | async-start | bytes 1146880 | tf_op jit(solution)/shard_map/reduce_scatter | solution.py:104
  234.2 20.6 %copy-start.8 = (f32[7,8,8,128]{3,2,1,0:T(8,128)}, f32[7,8,8,128]{3,2,1,0:T(8,128)S(1)}, u32[]{:S(2)}) copy-start(f32[7,8,8,128]{3,2,1,0:T(8,128)S(1)} %copy.55) | copy-start | bytes 688132
  295.8 7.3 %copy-start.4 = (bf16[32,24,2048]{2,1,0:T(8,128)(2,1)S(1)}, bf16[32,24,2048]{2,1,0:T(8,128)(2,1)}, u32[]{:S(2)}) copy-start(bf16[32,24,2048]{2,1,0:T(8,128)(2,1)} %copy-done.3) | copy-start | bytes 9437188
  306.7 71.9 %copy-start.12 = (f32[224,224]{1,0:T(8,128)S(1)}, f32[224,224]{1,0:T(8,128)}, u32[]{:S(2)}) copy-start(f32[224,224]{1,0:T(8,128)} %param.17) | copy-start | bytes 602116
  306.7 99.1 %copy-start.7 = (f32[56,1024]{1,0:T(8,128)S(1)}, f32[56,1024]{1,0:T(8,128)}, u32[]{:S(2)}) copy-start(f32[56,1024]{1,0:T(8,128)} %reduce-scatter.4.cloned.1.call-done) | copy-start | bytes 688132
  306.7 184.9 %copy-start.9 = (f32[7,8,8,128]{3,2,1,0:T(8,128)S(1)}, f32[7,8,8,128]{3,2,1,0:T(8,128)}, u32[]{:S(2)}) copy-start(f32[7,8,8,128]{3,2,1,0:T(8,128)} %copy-done.8) | copy-start | bytes 688132
  380.4 285.3 %reduce-scatter.8.cloned.1.call-start = ((), (), s32[]{:S(2)}) async-start(), calls=%async_computation.8 | async-start | bytes 1146880 | tf_op jit(solution)/shard_map/reduce_scatter | solution.py:104
  407.4 84.2 %copy-start.11 = (f32[56,1024]{1,0:T(8,128)}, f32[56,1024]{1,0:T(8,128)S(1)}, u32[]{:S(2)}) copy-start(f32[56,1024]{1,0:T(8,128)S(1)} %get-tuple-element.10) | copy-start | bytes 688132
  449.2 42.4 %copy-start.10 = (f32[7,8,8,128]{3,2,1,0:T(8,128)}, f32[7,8,8,128]{3,2,1,0:T(8,128)S(1)}, u32[]{:S(2)}) copy-start(f32[7,8,8,128]{3,2,1,0:T(8,128)S(1)} %copy.58) | copy-start | bytes 688132
  552.7 7.3 %copy-start.5 = (bf16[32,24,2048]{2,1,0:T(8,128)(2,1)S(1)}, bf16[32,24,2048]{2,1,0:T(8,128)(2,1)}, u32[]{:S(2)}) copy-start(bf16[32,24,2048]{2,1,0:T(8,128)(2,1)} %copy-done.3) | copy-start | bytes 9437188
  563.5 147.1 %copy-start.1 = (bf16[768,2048]{1,0:T(8,128)(2,1)S(1)}, bf16[768,2048]{1,0:T(8,128)(2,1)}, u32[]{:S(2)}) copy-start(bf16[768,2048]{1,0:T(8,128)(2,1)} %param.9) | copy-start | bytes 9437188
Sparse Core Ops, SparseCore 0:
  207.7 25.4 reduce-scatter.3
  380.6 25.1 reduce-scatter.5
  639.7 25.9 reduce-scatter.7
where the time goes:
time: 725 us; the launch traced here: 718 us
  other arithmetic  231 us (32%)
  blocking collectives  157 us (22%)
  waiting for transfers between devices  149 us (21%)
  local copies, waits for them, and re-layouts  136 us (19%)
  between operations  19.3 us (3%)
  starting transfers between devices  16.4 us (2%)
  matrix products  9.64 us (1%)
    scatter-add x3, other arithmetic, spread(): jnp.zeros((time_dev * reg_dev, cell_count), jnp.float32).at[index]  199 us
    psum x3, blocking collectives, inner(): return lax.psum(jnp.sum(first * second), ('region', 'tm'))  119 us
    gather x4, local copies, waits for them, and re-layouts, observe(): slab = field.reshape(time_dev * reg_dev, cell_count)[index]  96.6 us
    reduce_scatter x3, waiting for transfers between devices, widen(): lax.psum_scatter(jnp.dot(block.T, scaled, precision=lax.Precision.HIGHEST...  76.9 us
    all_to_all x1, waiting for transfers between devices, local(): lax.all_to_all(rows_out, ('region', 'tm'), split_axis=0, concat_axis=0, t...  68.4 us
    all_gather x2, blocking collectives, narrow(): piece = lax.all_gather(field, 'tm', axis=0, tiled=True)  38 us
    mul x3, other arithmetic, spread(): terms = shaped.astype(jnp.float32) * values[:, None, None]  16 us
  transfers between devices with their start and end apart: 6, of which 5 were waited for; matrix products, arithmetic and copies ran while one was open for 2% of the time, Pallas kernels for 0%

commit v1 on v0

v1 whole, which is shorter than its diff:
```python
import functools

import jax
import jax.numpy as jnp
from jax import lax
from jax.experimental import pallas as pl
from jax.experimental.pallas import tpu as pltpu
from jax.sharding import PartitionSpec as P

F32 = jnp.float32
BF16 = jnp.bfloat16
LANES = 128
VMEM_LIMIT = 40 << 20
META = 8


class Dims:
    def __init__(self, jacobian, kept_list, prior_std, regions, windows):
        self.regions = regions
        self.windows = windows
        self.devices = regions * windows
        self.time_dev, self.blocks, self.cells = prior_std.shape
        self.pool = jacobian.shape[0]
        self.keep = kept_list.shape[0]
        self.lag = jacobian.shape[1] // self.cells
        self.times = self.time_dev * windows
        self.cap = 3 * self.keep // (2 * self.devices)
        self.slice = self.cells // windows
        self.group = LANES // self.slice
        self.tiles = self.lag // self.group
        self.width = self.lag * self.slice
        self.slots = self.devices * self.cap
        self.piece = windows * self.cap
        self.rows = self.piece + META
        self.offsets = -(-(self.time_dev - self.lag + 1) // 16) * 16
        self.places = self.offsets * self.blocks
        self.halves = self.blocks // self.group
        self.packed = self.halves * LANES
        assert self.cells == LANES and self.blocks == 8 and self.group == windows


def iota(shape, axis):
    return lax.broadcasted_iota(jnp.int32, shape, axis)


def onehot(match):
    return jnp.where(match, 1.0, 0.0).astype(BF16)


def dot(a, b, contract=(1, 0)):
    return lax.dot_general(
        a, b, (((contract[0],), (contract[1],)), ((), ())), preferred_element_type=F32
    )


def halves(x):
    high = x.astype(BF16)
    return high, (x - high.astype(F32)).astype(BF16)


def dot3(a, b):
    ah, al = halves(a)
    bh, bl = halves(b)
    return dot(ah, bh) + (dot(ah, bl) + dot(al, bh))


def group_of(shape, d):
    return iota(shape, 1) >> (d.slice.bit_length() - 1)


def everywhere(x, d):
    shift = LANES // 2
    while shift >= d.slice:
        x = x + pltpu.roll(x, shift, 1)
        shift //= 2
    return x


def params(**kw):
    return pltpu.CompilerParams(vmem_limit_bytes=VMEM_LIMIT, **kw)


def vmem():
    return pl.BlockSpec(memory_space=pltpu.VMEM)


def smem():
    return pl.BlockSpec(memory_space=pltpu.SMEM)


def pack_body(d, count_ref, list_ref, block_ref, time_ref, weight_ref, misfit_ref, jac_ref,
              out_ref, select_ref, meta_ref):
    step = pl.program_id(0)

    @pl.when(step == 0)
    def _():
        listed = jnp.broadcast_to(list_ref[...], (d.pool, d.keep))
        live = iota((d.pool, d.keep), 1) < count_ref[0]
        hit = onehot((iota((d.pool, d.keep), 0) == listed) & live)
        kept = dot(jnp.ones((16, d.keep), BF16), hit, (1, 1))[0:1] > 0.5
        block = block_ref[...]
        time = time_ref[...]
        window = jnp.zeros_like(time)
        for w in range(1, d.windows):
            window += jnp.where(time >= w * d.time_dev, 1, 0)
        target = (block >> 3) * d.windows + window
        target = jnp.where(kept, target, -1)
        mine = iota((d.devices, d.pool), 0) == jnp.broadcast_to(target, (d.devices, d.pool))
        before = onehot(iota((d.pool, d.pool), 0) < iota((d.pool, d.pool), 1))
        ranks = dot(onehot(mine), before)
        rank = jnp.sum(jnp.where(mine, ranks, 0.0), axis=0, keepdims=True).astype(jnp.int32)
        slot = jnp.where(kept, target * d.cap + rank, -1)
        select = onehot(iota((d.slots, d.pool), 0) == jnp.broadcast_to(slot, (d.slots, d.pool)))
        select_ref[...] = select
        row = iota((16, d.pool), 0)
        fields = jnp.where(row == 0, (block & 7).astype(F32), 0.0)
        fields = jnp.where(row == 1, (time - window * d.time_dev).astype(F32), fields)
        fields = jnp.where(row == 2, weight_ref[...].astype(F32), fields)
        fields = jnp.where(row == 3, misfit_ref[...].astype(F32), fields)
        fields = jnp.where(row == 4, 1.0, fields)
        meta_ref[...] = dot(fields.astype(BF16), select, (1, 1))[0:META]

    wide = d.group * LANES
    a, b = iota((wide, wide), 0), iota((wide, wide), 1)
    bits = d.slice.bit_length() - 1
    cell = a & (LANES - 1)
    place = ((cell >> bits) << 7) + ((a >> 7) << bits) + (cell & (d.slice - 1))
    turn = onehot(place == b)
    rows = dot(select_ref[...], jac_ref[...]).astype(BF16)
    turned = dot(rows, turn).astype(BF16)
    for r in range(d.regions):
        low = r * d.piece
        shifted = pltpu.roll(meta_ref[...], (d.slots - low) % d.slots, 1)[:, :LANES]
        meta = jnp.where(step == 0, shifted, 0.0).astype(BF16)
        for j in range(d.windows):
            out_ref[r, j, 0:d.piece, :] = turned[low:low + d.piece, j * LANES:(j + 1) * LANES]
            out_ref[r, j, d.piece:d.rows, :] = meta


def pack(d, count, listed, block, time, weight, misfit, jacobian):
    wide = d.group * LANES
    whole = lambda n: pl.BlockSpec((1, n), lambda g: (0, 0))
    return pl.pallas_call(
        functools.partial(pack_body, d),
        name="pack",
        grid=(d.tiles,),
        in_specs=[smem(), whole(d.keep)] + [whole(d.pool)] * 4
        + [pl.BlockSpec((d.pool, wide), lambda g: (0, g))],
        out_specs=pl.BlockSpec((d.regions, d.windows, d.rows, LANES), lambda g: (0, 0, 0, g)),
        out_shape=jax.ShapeDtypeStruct((d.regions, d.windows, d.rows, d.width), BF16),
        scratch_shapes=[pltpu.VMEM((d.slots, d.pool), BF16), pltpu.VMEM((META, d.slots), F32)],
        compiler_params=params(),
    )(count, listed[None], block[None], time[None], weight[None], misfit[None], jacobian)


def prior_body(d, me_ref, prior_ref, out_ref):
    me = me_ref[0]
    lane = group_of((d.time_dev, LANES), d)
    for h in range(d.halves):
        rows = [prior_ref[pl.ds(h * d.group + m, d.time_dev, stride=d.blocks), :] for m in range(d.group)]
        for s in range(d.windows):
            to = me ^ s
            total = jnp.zeros((d.time_dev, LANES), F32)
            for m in range(d.group):
                turn = (m - to + d.group) % d.group * d.slice
                total = jnp.where(lane == m, pltpu.roll(rows[m], turn, 1), total)
            out_ref[s, :, h * LANES:(h + 1) * LANES] = total


def split_prior(d, me, prior):
    return pl.pallas_call(
        functools.partial(prior_body, d),
        name="split_prior",
        in_specs=[smem(), vmem()],
        out_specs=vmem(),
        out_shape=jax.ShapeDtypeStruct((d.windows, d.time_dev, d.packed), F32),
        compiler_params=params(),
    )(me, prior.reshape(d.time_dev * d.blocks, LANES))


def join_body(d, me_ref, *refs):
    pieces, outs = refs[:d.windows], refs[d.windows:]
    me = me_ref[0]
    lane = group_of((d.time_dev, LANES), d)
    for k, out_ref in enumerate(outs):
        for h in range(d.halves):
            tiles = [p[k, :, h * LANES:(h + 1) * LANES] for p in pieces]
            for m in range(d.group):
                total = jnp.zeros((d.time_dev, LANES), F32)
                for s in range(d.windows):
                    source = me ^ s
                    turn = (source - m + d.group) % d.group * d.slice
                    total = jnp.where(lane == source, pltpu.roll(tiles[s], turn, 1), total)
                out_ref[pl.ds(h * d.group + m, d.time_dev, stride=d.blocks), :] = total


def join(d, me, pieces):
    flat = jax.ShapeDtypeStruct((d.time_dev * d.blocks, LANES), F32)
    outs = pl.pallas_call(
        functools.partial(join_body, d),
        name="join",
        in_specs=[smem()] + [vmem()] * d.windows,
        out_specs=[vmem()] * 2,
        out_shape=[flat, flat],
        compiler_params=params(),
    )(me, *pieces)
    return tuple(o.reshape(d.time_dev, d.blocks, LANES) for o in outs)


FRONT = 8
CHUNK = 16


def transpose_rows(d, row):
    return jnp.broadcast_to(row, (LANES, d.slots)).T


def spread(d, values, rows_ref, place_t_ref, std_ref, sum_ref, field_ref, packed_ref):
    sum_ref[...] = jnp.zeros_like(sum_ref)
    for w in range(d.windows):
        high, low = halves(values[w:w + 1])
        place = place_t_ref[w]
        rows = rows_ref[w]
        total = dot(place * high, rows) + dot(place * low, rows)
        for g in range(d.tiles):
            start = (FRONT + w * d.time_dev + d.group * g) * d.blocks
            sum_ref[start:start + d.places, :] += total[:, g * LANES:(g + 1) * LANES]
    size = CHUNK * d.blocks
    lane = group_of((size, LANES), d)

    @pl.loop(0, d.times // CHUNK)
    def _(i):
        start = pl.multiple_of(i * size, size)
        x = sum_ref[pl.ds(start + FRONT * d.blocks, size), :]
        for m in range(1, d.group):
            x = jnp.where(lane == m, sum_ref[pl.ds(start + (FRONT - m) * d.blocks, size), :], x)
        field_ref[pl.ds(start, size), :] = everywhere(x, d) * std_ref[pl.ds(start, size), :]

    lane = group_of((d.times, LANES), d)
    for h in range(d.halves):
        x = field_ref[pl.ds(h * d.group, d.times, stride=d.blocks), :]
        for m in range(1, d.group):
            x = jnp.where(lane == m, field_ref[pl.ds(h * d.group + m, d.times, stride=d.blocks), :], x)
        packed_ref[:, h * LANES:(h + 1) * LANES] = x


def unpack(d, packed, field_ref):
    lane = group_of((d.times, LANES), d)
    for h in range(d.halves):
        tile = packed[:, h * LANES:(h + 1) * LANES]
        for m in range(d.group):
            x = everywhere(jnp.where(lane == m, tile, 0.0), d)
            field_ref[pl.ds(h * d.group + m, d.times, stride=d.blocks), :] = x


def observe(d, mix_ref, packed_ref, rows_ref, place_ref, std_ref, field_ref, high_ref, low_ref, out_ref):
    unpack(d, dot3(mix_ref[...], packed_ref[...]), field_ref)
    size = CHUNK * d.blocks
    tail = 2 * CHUNK * d.blocks
    field_ref[pl.ds(d.times * d.blocks, tail), :] = jnp.zeros((tail, LANES), F32)

    @pl.loop(0, d.times // CHUNK)
    def _(i):
        start = pl.multiple_of(i * size, size)
        field_ref[pl.ds(start, size), :] = field_ref[pl.ds(start, size), :] * std_ref[pl.ds(start, size), :]

    lane = group_of((size, LANES), d)

    @pl.loop(0, d.times // CHUNK + 1)
    def _(i):
        start = pl.multiple_of(i * size, size)
        x = field_ref[pl.ds(start, size), :]
        for m in range(1, d.group):
            x = jnp.where(lane == m, field_ref[pl.ds(start + m * d.blocks, size), :], x)
        high, low = halves(x)
        high_ref[pl.ds(start, size), :] = high
        low_ref[pl.ds(start, size), :] = low

    for w in range(d.windows):
        starts = [(w * d.time_dev + d.group * g) * d.blocks for g in range(d.tiles)]
        high = jnp.concatenate([high_ref[s:s + d.places, :] for s in starts], axis=1)
        low = jnp.concatenate([low_ref[s:s + d.places, :] for s in starts], axis=1)
        place = place_ref[w]
        product = rows_ref[w].astype(F32) * (dot(place, high) + dot(place, low))
        part = product[:, :LANES]
        for g in range(1, d.tiles):
            part = part + product[:, g * LANES:(g + 1) * LANES]
        out_ref[w:w + 1, :] = jnp.sum(part.T, axis=0, keepdims=True)


def work_shapes(d):
    return [
        pltpu.VMEM(((FRONT + d.times + CHUNK) * d.blocks, LANES), F32),
        pltpu.VMEM(((d.times + 2 * CHUNK) * d.blocks, LANES), F32),
        pltpu.VMEM(((d.times + CHUNK) * d.blocks, LANES), BF16),
        pltpu.VMEM(((d.times + CHUNK) * d.blocks, LANES), BF16),
    ]


def first_body(d, me_ref, got_ref, mix_ref, *refs):
    stds = refs[:d.windows]
    (rows_ref, place_t_ref, place_ref, std_ref, weight_ref, value_ref, packed_ref, seen_ref,
     wide_ref, stdp_ref, sum_ref, field_ref, high_ref, low_ref) = refs[d.windows:]
    me = me_ref[0]
    for s in range(d.devices):
        x = got_ref[s, 0:d.piece, :].astype(F32)
        for w in range(d.windows):
            wide_ref[w, s * d.cap:(s + 1) * d.cap, :] = x[w * d.cap:(w + 1) * d.cap, :]
    for w in range(d.windows):
        rows_ref[w] = wide_ref[w].astype(BF16)
    count = d.slots // LANES
    lane = iota((META, LANES), 1)
    meta = [[jnp.zeros((META, LANES), F32)] * count for _ in range(d.windows)]
    for s in range(d.devices):
        m = got_ref[s, d.piece:d.rows, 0:LANES].astype(F32)
        low, high = s * d.cap, (s + 1) * d.cap
        for w in range(d.windows):
            turned = pltpu.roll(m, (low - w * d.cap) % LANES, 1)
            for tile in range(low // LANES, (high - 1) // LANES + 1):
                here = (lane + tile * LANES >= low) & (lane + tile * LANES < high)
                meta[w][tile] = jnp.where(here, turned, meta[w][tile])
    for w in range(d.windows):
        fields = jnp.concatenate(meta[w], axis=1)
        key = jnp.where(fields[4:5] > 0.5, fields[1:2] * d.blocks + fields[0:1], -1.0)
        number = key.astype(jnp.int32)
        place_t_ref[w] = onehot(iota((d.places, d.slots), 0) == jnp.broadcast_to(number, (d.places, d.slots)))
        column = transpose_rows(d, key).astype(jnp.int32)
        for k in range(d.places // LANES):
            place_ref[w, :, k * LANES:(k + 1) * LANES] = onehot(iota((d.slots, LANES), 1) + k * LANES == column)
        weight_ref[w:w + 1, :] = fields[2:3]
        value_ref[w:w + 1, :] = fields[2:3] * fields[3:4]
    for s in range(d.windows):
        stdp_ref[pl.ds(pl.multiple_of((me ^ s) * d.time_dev, 8), d.time_dev), :] = stds[s][...]
    unpack(d, stdp_ref[...], std_ref)
    spread(d, value_ref[...], rows_ref, place_t_ref, std_ref, sum_ref, field_ref, packed_ref)
    observe(d, mix_ref, packed_ref, rows_ref, place_ref, std_ref, field_ref, high_ref, low_ref, seen_ref)


def first(d, me, got, mix, stds):
    per_slot = jax.ShapeDtypeStruct((d.windows, d.slots), F32)
    return pl.pallas_call(
        functools.partial(first_body, d),
        name="first",
        in_specs=[smem()] + [vmem()] * (2 + d.windows),
        out_specs=[vmem()] * 8,
        out_shape=[
            jax.ShapeDtypeStruct((d.windows, d.slots, d.width), BF16),
            jax.ShapeDtypeStruct((d.windows, d.places, d.slots), BF16),
            jax.ShapeDtypeStruct((d.windows, d.slots, d.places), BF16),
            jax.ShapeDtypeStruct((d.times * d.blocks, LANES), F32),
            per_slot,
            per_slot,
            jax.ShapeDtypeStruct((d.times, d.packed), F32),
            per_slot,
        ],
        scratch_shapes=[
            pltpu.VMEM((d.windows, d.slots, d.width), F32),
            pltpu.VMEM((d.times, d.packed), F32),
        ] + work_shapes(d),
        compiler_params=params(),
    )(me, got, mix, *stds)


def total_of(x):
    return jnp.sum(jnp.sum(x, axis=0, keepdims=True), axis=1, keepdims=True)


def write_moments(out_ref, numbers):
    row = iota((8, LANES), 0)
    x = jnp.zeros((8, LANES), F32)
    for k, number in enumerate(numbers):
        x = jnp.where(row == k, jnp.broadcast_to(number, (8, LANES)), x)
    out_ref[...] = x


def second_body(d, rows_ref, place_t_ref, place_ref, std_ref, mix_ref, weight_ref, value_ref, *refs):
    parts = refs[:d.windows]
    (next_ref, packed_ref, seen_ref, moment_ref, sum_ref, field_ref, high_ref, low_ref) = refs[d.windows:]
    seen = parts[0][...]
    for p in parts[1:]:
        seen = seen + p[...]
    next_ref[...] = weight_ref[...] * seen
    write_moments(moment_ref, [total_of(value_ref[...] * seen), total_of(next_ref[...] * seen)])
    spread(d, next_ref[...], rows_ref, place_t_ref, std_ref, sum_ref, field_ref, packed_ref)
    observe(d, mix_ref, packed_ref, rows_ref, place_ref, std_ref, field_ref, high_ref, low_ref, seen_ref)


def second(d, rows, place_t, place, std, mix, weight, value, parts):
    per_slot = jax.ShapeDtypeStruct((d.windows, d.slots), F32)
    return pl.pallas_call(
        functools.partial(second_body, d),
        name="second",
        in_specs=[vmem()] * (7 + d.windows),
        out_specs=[vmem()] * 4,
        out_shape=[
            per_slot,
            jax.ShapeDtypeStruct((d.times, d.packed), F32),
            per_slot,
            jax.ShapeDtypeStruct((8, LANES), F32),
        ],
        scratch_shapes=work_shapes(d),
        compiler_params=params(),
    )(rows, place_t, place, std, mix, weight, value, *parts)


def third_body(d, weight_ref, value_ref, before_ref, *refs):
    parts = refs[:d.windows]
    next_ref, moment_ref = refs[d.windows:]
    seen = parts[0][...]
    for p in parts[1:]:
        seen = seen + p[...]
    next_ref[...] = weight_ref[...] * seen
    old = before_ref[...]
    write_moments(
        moment_ref,
        [old[0:1], old[1:2], total_of(value_ref[...] * seen), total_of(next_ref[...] * seen)],
    )


def third(d, weight, value, before, parts):
    return pl.pallas_call(
        functools.partial(third_body, d),
        name="third",
        in_specs=[vmem()] * (3 + d.windows),
        out_specs=[vmem()] * 2,
        out_shape=[
            jax.ShapeDtypeStruct((d.windows, d.slots), F32),
            jax.ShapeDtypeStruct((8, LANES), F32),
        ],
        compiler_params=params(),
    )(weight, value, before, *parts)


def fourth_body(d, value_ref, rows_ref, place_t_ref, std_ref, packed_ref, sum_ref, field_ref):
    spread(d, value_ref[...], rows_ref, place_t_ref, std_ref, sum_ref, field_ref, packed_ref)


def fourth(d, value, rows, place_t, std):
    return pl.pallas_call(
        functools.partial(fourth_body, d),
        name="fourth",
        in_specs=[vmem()] * 4,
        out_specs=vmem(),
        out_shape=jax.ShapeDtypeStruct((d.times, d.packed), F32),
        scratch_shapes=work_shapes(d)[:2],
        compiler_params=params(),
    )(value, rows, place_t, std)


def last_body(d, me_ref, moment_ref, factor_ref, a_ref, b_ref, c_ref, out_ref, hold_ref):
    me = me_ref[0]
    m0, m1, m2, m3 = (moment_ref[k:k + 1, :] for k in range(4))
    alpha0 = m0 / (m0 + m1)
    p, q = 1.0 - alpha0, -alpha0
    norm = p * p * m0 + 2.0 * p * q * m1 + q * q * m2
    e = p + norm / m0
    cross = (e * e * m0 + 2.0 * e * q * m1 + q * q * m2) + (e * e * m1 + 2.0 * e * q * m2 + q * q * m3)
    alpha1 = norm / cross
    for h in range(d.halves):
        low, high = h * LANES, (h + 1) * LANES
        a, b, c = a_ref[:, low:high], b_ref[:, low:high], c_ref[:, low:high]
        x = (alpha0 + alpha1 * e) * a + (alpha1 * q) * b
        r = (p - alpha1 * e) * a + (q - alpha1 * (e + q)) * b - (alpha1 * q) * c
        for k, v in enumerate((x, r)):
            fh, fl = halves(factor_ref[...])
            vh, vl = halves(v)
            y = dot(fh, vh, (0, 0)) + (dot(fh, vl, (0, 0)) + dot(fl, vh, (0, 0)))
            hold_ref[k, :, low:high] = y
    for s in range(d.windows):
        start = pl.multiple_of((me ^ s) * d.time_dev, 8)
        for k in range(2):
            out_ref[s, k] = hold_ref[k, pl.ds(start, d.time_dev), :]


def last(d, me, moments, factor, a, b, c):
    return pl.pallas_call(
        functools.partial(last_body, d),
        name="last",
        in_specs=[smem()] + [vmem()] * 5,
        out_specs=vmem(),
        out_shape=jax.ShapeDtypeStruct((d.windows, 2, d.time_dev, d.packed), F32),
        scratch_shapes=[pltpu.VMEM((2, d.times, d.packed), F32)],
        compiler_params=params(),
    )(me, moments, factor, a, b, c)


def swap(x, axis, step):
    size = lax.axis_size(axis)
    return lax.ppermute(x, axis, [(k, k ^ step) for k in range(size)])


def share(d, x):
    return [x] + [swap(x, "tm", s) for s in range(1, d.windows)]


def local(
    jacobian,
    foot_block,
    foot_time,
    obs_weight,
    misfit,
    kept_list,
    kept_count,
    prior_std,
    time_factor,
):
    d = Dims(jacobian, kept_list, prior_std, lax.axis_size("region"), lax.axis_size("tm"))
    me = lax.axis_index("tm").astype(jnp.int32).reshape(1)
    mix = jnp.dot(time_factor, time_factor.T, precision=lax.Precision.HIGHEST)
    ours = split_prior(d, me, prior_std)
    stds = [ours[0]] + [swap(ours[s], "tm", s) for s in range(1, d.windows)]
    pieces = pack(d, kept_count, kept_list, foot_block, foot_time, obs_weight, misfit, jacobian)
    got = lax.all_to_all(
        pieces.reshape(d.devices, d.rows, d.width), ("region", "tm"), split_axis=0, concat_axis=0, tiled=True
    )
    rows, place_t, place, std, weight, value0, u0, seen0 = first(d, me, got, mix, stds)
    value1, u1, seen1, early = second(d, rows, place_t, place, std, mix, weight, value0, share(d, seen0))
    value2, moments = third(d, weight, value1, early, share(d, seen1))
    u2 = fourth(d, value2, rows, place_t, std)
    step = 1
    while step < d.regions:
        moments = moments + swap(moments, "region", step)
        step *= 2
    both = last(d, me, moments, time_factor, u0, u1, u2)
    parts = [both[0]] + [swap(both[s], "tm", s) for s in range(1, d.windows)]
    return join(d, me, parts)


def solution(mesh):
    return jax.shard_map(
        local,
        mesh=mesh,
        in_specs=(
            P(("region", "tm"), None),
            P(("region", "tm")),
            P(("region", "tm")),
            P(("region", "tm")),
            P(("region", "tm")),
            P(("region", "tm")),
            P(("region", "tm")),
            P("tm", "region", None),
            P(),
        ),
        out_specs=(P("tm", "region", None), P("tm", "region", None)),
        check_vma=False,
    )
```

time: 725 us -> 169 us (0.23)
  other arithmetic: 231 us -> 0.01 us
  blocking collectives: 157 us -> 0 us
  local copies, waits for them, and re-layouts: 136 us -> 11.8 us
  waiting for transfers between devices: 149 us -> 92.1 us
  Pallas kernels: 0 us -> 34.4 us
  between operations: 19.3 us -> 1.41 us
  starting transfers between devices: 16.4 us -> 26.6 us
  matrix products: 9.64 us -> 2.12 us
    scatter-add x3 -> x0, other arithmetic: 199 us -> none  [spread(): jnp.zeros((time_dev * reg_dev, cell_count), jnp.float32).at[index]]
    psum x3 -> x0, blocking collectives: 119 us -> none  [inner(): return lax.psum(jnp.sum(first * second), ('region', 'tm'))]
    gather x8 -> x0, local copies, waits for them, and re-layouts: 111 us -> none  [the longest x4 96.6 us: observe(): slab = field.reshape(time_dev * reg_dev, cell_count)[index]]
    ppermute x0 -> x15, waiting for transfers between devices: none -> 92.1 us  [swap(): return lax.ppermute(x, axis, [(k, k ^ step) for k in range(size)])]
    reduce_scatter x3 -> x0, waiting for transfers between devices: 76.9 us -> none  [widen(): lax.psum_scatter(jnp.dot(block.T, scaled, precision=lax.Precision.HIGHEST...]
    all_to_all x3 -> x1, waiting for transfers between devices: 71.5 us -> 0.01 us  [local(): lax.all_to_all(pieces.reshape(d.devices, d.rows, d.width), ('region', 'tm...]
    all_gather x2 -> x0, blocking collectives: 38 us -> none  [narrow(): piece = lax.all_gather(field, 'tm', axis=0, tiled=True)]
    pallas_call x0 -> x8, Pallas kernels: none -> 34.4 us  [the longest x1 10.5 us: first(): pl.pallas_call(functools.partial(first_body, d), name='first', in_specs=[...]
  transfers between devices with their start and end apart: 6 -> 16, of which waited for: 5 -> 11; matrix products, arithmetic and copies ran while one was open for 2% -> 1% of each run, Pallas kernels for 0% -> 3%
where the time goes in v1:
time: 169 us
  waiting for transfers between devices  92.1 us (54%)
  Pallas kernels  34.4 us (20%)
  starting transfers between devices  26.6 us (16%)
  local copies, waits for them, and re-layouts  11.8 us (7%)
  matrix products  2.12 us (1%)
    ppermute x15, waiting for transfers between devices, swap(): return lax.ppermute(x, axis, [(k, k ^ step) for k in range(size)])  92.1 us
    ppermute x15, starting transfers between devices, swap(): return lax.ppermute(x, axis, [(k, k ^ step) for k in range(size)])  19.3 us
    pallas_call x1, Pallas kernels, first(): pl.pallas_call(functools.partial(first_body, d), name='first', in_specs=[...  10.5 us
    pallas_call x1, Pallas kernels, second(): pl.pallas_call(functools.partial(second_body, d), name='second', in_specs...  9.95 us
    unnamed x20, local copies, waits for them, and re-layouts  9.03 us
    all_to_all x1, starting transfers between devices, local(): lax.all_to_all(pieces.reshape(d.devices, d.rows, d.width), ('region', 'tm...  7.32 us
    pallas_call x1, Pallas kernels, pack(): pl.pallas_call(functools.partial(pack_body, d), name='pack', grid=(d.tile...  6.8 us
    pallas_call x1, Pallas kernels, fourth(): pl.pallas_call(functools.partial(fourth_body, d), name='fourth', in_specs...  4.95 us
  transfers between devices with their start and end apart: 16, of which 11 were waited for; matrix products, arithmetic and copies ran while one was open for 1% of the time, Pallas kernels for 3%

profile of v1, /device:TPU:0, one launch (start us, length us, event | category | flops | bytes accessed | tf_op | source)
XLA Modules:
  0.0 168.5 jit_solution(13818027245423012092)
XLA Ops:
  1.3 0.7 broadcast_in_dim.16.block_ref
  2.0 0.7 broadcast_in_dim.17.time_ref
  2.7 0.7 broadcast_in_dim.18.weight_ref
  3.3 0.7 broadcast_in_dim.19.misfit_ref
  4.0 1.9 %copy-done.1 = bf16[768,2048]{1,0:T(8,128)(2,1)S(1)} copy-done((bf16[768,2048]{1,0:T(8,128)(2,1)S(1)}, bf16[768,2048]{1,0:T(8,128)(2,1)}, u32[]{:S(2)}) %copy-start.1) | copy-done | bytes 3145752
  5.9 0.7 copy-done.9
  6.6 6.8 %pack.1 = bf16[8,4,104,512]{3,2,1,0:T(8,128)(2,1)S(1)} custom-call(s32[1]{0:T(128)S(6)} %copy.11.count_ref, s32[1,512]{1,0:T(1,128)S(1)} %bitcast.26, s32[1,768]{1,0:T(1,128)S(1)} %broadcast_in_dim.16.block_ref, s32[1,768]{1,0:T(1,128)S(1)} %broadcast_in_dim.17.time_ref, bf16[1,768]{1,0:T(2,128)(2,1)S(1)} %broadcast_in_dim.18.weight_ref, ...), custom_call_target="tpu_custom_call" | custom-call | tf_op jit(solution)/shard_map/pack/pallas_call | solution.py:143
  13.4 1.7 %copy-done = bf16[8,4,104,512]{3,2,1,0:T(8,128)(2,1)} copy-done((bf16[8,4,104,512]{3,2,1,0:T(8,128)(2,1)}, bf16[8,4,104,512]{3,2,1,0:T(8,128)(2,1)S(1)}, u32[]{:S(2)}) %copy-start) | copy-done | bytes 3407896
  15.1 7.3 %all-to-all-start = ((bf16[32,104,512]{2,1,0:T(8,128)(2,1)}), bf16[32,104,512]{2,1,0:T(8,128)(2,1)S(1)}, u32[]{:S(2)}, u32[]{:S(2)}) async-start(bf16[32,104,512]{2,1,0:T(8,128)(2,1)} %bitcast.24), calls=%async_computation | async-start | bytes 6815744 | tf_op jit(solution)/shard_map/all_to_all | solution.py:513
  22.5 0.0 copy-start.4
  22.5 0.9 copy-done.4
  23.4 0.3 split_prior.1
  23.7 3.7 %collective-permute-start.2 = (f32[56,256]{1,0:T(8,128)S(1)}, f32[56,256]{1,0:T(8,128)S(1)}, u32[]{:S(2)}, u32[]{:S(2)}) collective-permute-start(f32[56,256]{1,0:T(8,128)S(1)} %get-tuple-element.38), channel_id=1, source_target_pairs={{0,3},{1,2},{2,1},{3,0},{4,7},{5,6},{6,5},{7,4},{8,11},{9,10},{10,... | collective-permute-start | bytes 172040 | tf_op jit(solution)/shard_map/ppermute | solution.py:489
  27.4 0.0 collective-permute-start.1
  27.4 0.8 collective-permute-start
  28.2 2.1 %fusion.mix_ref = f32[224,224]{1,0:T(8,128)} fusion(f32[224,224]{1,0:T(8,128)} %factor_ref.1), kind=kOutput, calls=%fused_computation.8 | convolution fusion | flops 134873088 | bytes 401408 | tf_op jit(solution)/shard_map/dot_general | solution.py:509
  30.3 54.7 %collective-permute-done.2.refs_3_ = f32[56,256]{1,0:T(8,128)S(1)} collective-permute-done((f32[56,256]{1,0:T(8,128)S(1)}, f32[56,256]{1,0:T(8,128)S(1)}, u32[]{:S(2)}, u32[]{:S(2)}) %collective-permute-start.2) | collective-permute-done | bytes 57376 | tf_op jit(solution)/shard_map/ppermute | solution.py:489
  85.0 20.8 %collective-permute-done.1.refs_2_ = f32[56,256]{1,0:T(8,128)S(1)} collective-permute-done((f32[56,256]{1,0:T(8,128)S(1)}, f32[56,256]{1,0:T(8,128)S(1)}, u32[]{:S(2)}, u32[]{:S(2)}) %collective-permute-start.1) | collective-permute-done | bytes 57376 | tf_op jit(solution)/shard_map/ppermute | solution.py:489
  105.8 0.6 copy-done.5
  106.4 0.6 copy-done.7
  107.1 0.9 copy-done.3
  108.0 0.8 copy-done.6
  108.8 0.8 copy-done.8
  109.6 10.5 %first.1 = (bf16[4,768,512]{2,1,0:T(8,128)(2,1)S(1)}, bf16[4,384,768]{2,1,0:T(8,128)(2,1)S(1)}, bf16[4,768,384]{2,1,0:T(8,128)(2,1)S(1)}, f32[1792,128]{1,0:T(8,...) custom-call(s32[1]{0:T(128)} %bitcast.me_ref, ...), custom_call_target="tpu_custom_call" | custom-call | tf_op jit(solution)/shard_map/first/pallas_call | solution.py:341
  120.1 0.3 collective-permute-start.5
  120.4 1.2 collective-permute-start.4
  121.5 3.0 %collective-permute-start.3 = (f32[4,768]{1,0:T(4,128)S(1)}, f32[4,768]{1,0:T(4,128)S(1)}, u32[]{:S(2)}, u32[]{:S(2)}) collective-permute-start(f32[4,768]{1,0:T(4,128)S(1)} %get-tuple-element.24.refs_0_), channel_id=1, source_target_pairs={{0,1},{1,0},{2,3},{3,2},{4,5},{5,4},{6,7},{7,6},{8,9},{9,8},{10,11... | collective-permute-start | bytes 36872 | tf_op jit(solution)/shard_map/ppermute | solution.py:489
  124.6 1.1 collective-permute-done.5.refs_3_
  125.7 0.6 collective-permute-done.3.refs_1_
  126.2 10.0 %second.1 = (f32[4,768]{1,0:T(4,128)S(1)}, f32[224,256]{1,0:T(8,128)S(1)}, f32[4,768]{1,0:T(4,128)S(1)}, f32[8,128]{1,0:T(8,128)S(1)}) custom-call(bf16[4,768,512]{2,1,0:T(8,128)(2,1)S(1)} %get-tuple-element.19.rows_ref, bf16[4,384,768]{2,1,0:T(8,128)(2,1)S(1)} %get-tuple-element.20.place_t_ref, bf16[4,768,384]{2,1,0:T(8,128)(2,1)S(1)} %get-tuple-element.21.place_ref, ...), custom_call_target="tpu_custom_call" | custom-call | tf_op jit(solution)/shard_map/second/pallas_call | solution.py:390
  136.2 2.4 %collective-permute-start.8 = (f32[4,768]{1,0:T(4,128)S(1)}, f32[4,768]{1,0:T(4,128)S(1)}, u32[]{:S(2)}, u32[]{:S(2)}) collective-permute-start(f32[4,768]{1,0:T(4,128)S(1)} %get-tuple-element.27.refs_0_), channel_id=1, source_target_pairs={{0,3},{1,2},{2,1},{3,0},{4,7},{5,6},{6,5},{7,4},{8,11},{9,10},{10,... | collective-permute-start | bytes 36872 | tf_op jit(solution)/shard_map/ppermute | solution.py:489
  138.6 1.1 collective-permute-start.7
  139.7 0.9 collective-permute-start.6
  140.6 1.1 collective-permute-done.8.refs_3_
  141.7 1.5 collective-permute-done.7.refs_2_
  143.2 0.2 collective-permute-done.6.refs_1_
  143.4 0.1 third.1
  143.5 1.2 collective-permute-done.9
  144.7 3.6 %collective-permute-done.10 = f32[8,128]{1,0:T(8,128)S(1)} collective-permute-done((f32[8,128]{1,0:T(8,128)S(1)}, f32[8,128]{1,0:T(8,128)S(1)}, u32[]{:S(2)}, u32[]{:S(2)}) %collective-permute-start.10) | collective-permute-done | bytes 4128 | tf_op jit(solution)/shard_map/ppermute | solution.py:489
  148.3 1.5 collective-permute-start.11
  149.8 4.9 %fourth.1.c_ref = f32[224,256]{1,0:T(8,128)S(1)} custom-call(f32[4,768]{1,0:T(4,128)S(1)} %get-tuple-element.31.value_ref, bf16[4,768,512]{2,1,0:T(8,128)(2,1)S(1)} %get-tuple-element.19.rows_ref, bf16[4,384,768]{2,1,0:T(8,128)(2,1)S(1)} %get-tuple-element.20.place_t_ref, f32[1792,128]{1,0:T(8,128)S(1)} %get-tuple-element.22.std_ref), custom_call_target="tpu_custom_call" | custom-call | tf_op jit(solution)/shard_map/fourth/pallas_call | solution.py:439
  154.8 0.6 last.1
  155.5 1.4 collective-permute-start.14
  156.9 1.0 collective-permute-start.13
  157.9 2.0 %collective-permute-start.12 = (f32[2,56,256]{2,1,0:T(8,128)S(1)}, f32[2,56,256]{2,1,0:T(8,128)S(1)}, u32[]{:S(2)}, u32[]{:S(2)}) collective-permute-start(f32[2,56,256]{2,1,0:T(8,128)S(1)} %get-tuple-element.36), channel_id=1, source_target_pairs={{0,1},{1,0},{2,3},{3,2},{4,5},{5,4},{6,7},{7,6},{8,9},{9,8},{10,11... | collective-permute-start | bytes 344072 | tf_op jit(solution)/shard_map/ppermute | solution.py:489
  159.9 3.4 %collective-permute-done.14.refs_3_ = f32[2,56,256]{2,1,0:T(8,128)S(1)} collective-permute-done((f32[2,56,256]{2,1,0:T(8,128)S(1)}, f32[2,56,256]{2,1,0:T(8,128)S(1)}, u32[]{:S(2)}, u32[]{:S(2)}) %collective-permute-start.14) | collective-permute-done | bytes 114720 | tf_op jit(solution)/shard_map/ppermute | solution.py:489
  163.4 3.9 %collective-permute-done.13.refs_2_ = f32[2,56,256]{2,1,0:T(8,128)S(1)} collective-permute-done((f32[2,56,256]{2,1,0:T(8,128)S(1)}, f32[2,56,256]{2,1,0:T(8,128)S(1)}, u32[]{:S(2)}, u32[]{:S(2)}) %collective-permute-start.13) | collective-permute-done | bytes 114720 | tf_op jit(solution)/shard_map/ppermute | solution.py:489
  167.3 1.2 join.1
  (22 shorter events, 0.1 us)
Async XLA Ops:
  4.0 1.9 %copy-start.1 = (bf16[768,2048]{1,0:T(8,128)(2,1)S(1)}, bf16[768,2048]{1,0:T(8,128)(2,1)}, u32[]{:S(2)}) copy-start(bf16[768,2048]{1,0:T(8,128)(2,1)} %jac_ref.1) | copy-start | bytes 9437188
  5.9 0.7 copy-start.9
  13.4 1.7 %copy-start = (bf16[8,4,104,512]{3,2,1,0:T(8,128)(2,1)}, bf16[8,4,104,512]{3,2,1,0:T(8,128)(2,1)S(1)}, u32[]{:S(2)}) copy-start(bf16[8,4,104,512]{3,2,1,0:T(8,128)(2,1)S(1)} %pack.1) | copy-start | bytes 10223620
  15.1 91.9 %all-to-all-start = ((bf16[32,104,512]{2,1,0:T(8,128)(2,1)}), bf16[32,104,512]{2,1,0:T(8,128)(2,1)S(1)}, u32[]{:S(2)}, u32[]{:S(2)}) async-start(bf16[32,104,512]{2,1,0:T(8,128)(2,1)} %bitcast.24), calls=%async_computation | async-start | bytes 6815744 | tf_op jit(solution)/shard_map/all_to_all | solution.py:513
  22.5 0.9 copy-start.4
  23.7 61.2 %collective-permute-start.2 = (f32[56,256]{1,0:T(8,128)S(1)}, f32[56,256]{1,0:T(8,128)S(1)}, u32[]{:S(2)}, u32[]{:S(2)}) collective-permute-start(f32[56,256]{1,0:T(8,128)S(1)} %get-tuple-element.38), channel_id=1, source_target_pairs={{0,3},{1,2},{2,1},{3,0},{4,7},{5,6},{6,5},{7,4},{8,11},{9,10},{10,... | collective-permute-start | bytes 172040 | tf_op jit(solution)/shard_map/ppermute | solution.py:489
  27.4 78.4 %collective-permute-start.1 = (f32[56,256]{1,0:T(8,128)S(1)}, f32[56,256]{1,0:T(8,128)S(1)}, u32[]{:S(2)}, u32[]{:S(2)}) collective-permute-start(f32[56,256]{1,0:T(8,128)S(1)} %get-tuple-element.39), channel_id=1, source_target_pairs={{0,2},{1,3},{2,0},{3,1},{4,6},{5,7},{6,4},{7,5},{8,10},{9,11},{10,... | collective-permute-start | bytes 172040 | tf_op jit(solution)/shard_map/ppermute | solution.py:489
  27.4 79.0 %collective-permute-start = (f32[56,256]{1,0:T(8,128)S(1)}, f32[56,256]{1,0:T(8,128)S(1)}, u32[]{:S(2)}, u32[]{:S(2)}) collective-permute-start(f32[56,256]{1,0:T(8,128)S(1)} %get-tuple-element.40), channel_id=1, source_target_pairs={{0,1},{1,0},{2,3},{3,2},{4,5},{5,4},{6,7},{7,6},{8,9},{9,8},{10,11... | collective-permute-start | bytes 172040 | tf_op jit(solution)/shard_map/ppermute | solution.py:489
  105.8 0.6 copy-start.5
  106.4 0.6 copy-start.7
  107.1 0.9 copy-start.3
  108.0 0.8 copy-start.6
  108.8 0.8 copy-start.8
  120.1 5.6 %collective-permute-start.5 = (f32[4,768]{1,0:T(4,128)S(1)}, f32[4,768]{1,0:T(4,128)S(1)}, u32[]{:S(2)}, u32[]{:S(2)}) collective-permute-start(f32[4,768]{1,0:T(4,128)S(1)} %get-tuple-element.24.refs_0_), channel_id=1, source_target_pairs={{0,3},{1,2},{2,1},{3,0},{4,7},{5,6},{6,5},{7,4},{8,11},{9,10},{10,... | collective-permute-start | bytes 36872 | tf_op jit(solution)/shard_map/ppermute | solution.py:489
  120.4 5.3 %collective-permute-start.4 = (f32[4,768]{1,0:T(4,128)S(1)}, f32[4,768]{1,0:T(4,128)S(1)}, u32[]{:S(2)}, u32[]{:S(2)}) collective-permute-start(f32[4,768]{1,0:T(4,128)S(1)} %get-tuple-element.24.refs_0_), channel_id=1, source_target_pairs={{0,2},{1,3},{2,0},{3,1},{4,6},{5,7},{6,4},{7,5},{8,10},{9,11},{10,... | collective-permute-start | bytes 36872 | tf_op jit(solution)/shard_map/ppermute | solution.py:489
  121.5 4.7 %collective-permute-start.3 = (f32[4,768]{1,0:T(4,128)S(1)}, f32[4,768]{1,0:T(4,128)S(1)}, u32[]{:S(2)}, u32[]{:S(2)}) collective-permute-start(f32[4,768]{1,0:T(4,128)S(1)} %get-tuple-element.24.refs_0_), channel_id=1, source_target_pairs={{0,1},{1,0},{2,3},{3,2},{4,5},{5,4},{6,7},{7,6},{8,9},{9,8},{10,11... | collective-permute-start | bytes 36872 | tf_op jit(solution)/shard_map/ppermute | solution.py:489
  136.2 5.6 %collective-permute-start.8 = (f32[4,768]{1,0:T(4,128)S(1)}, f32[4,768]{1,0:T(4,128)S(1)}, u32[]{:S(2)}, u32[]{:S(2)}) collective-permute-start(f32[4,768]{1,0:T(4,128)S(1)} %get-tuple-element.27.refs_0_), channel_id=1, source_target_pairs={{0,3},{1,2},{2,1},{3,0},{4,7},{5,6},{6,5},{7,4},{8,11},{9,10},{10,... | collective-permute-start | bytes 36872 | tf_op jit(solution)/shard_map/ppermute | solution.py:489
  138.6 4.6 %collective-permute-start.7 = (f32[4,768]{1,0:T(4,128)S(1)}, f32[4,768]{1,0:T(4,128)S(1)}, u32[]{:S(2)}, u32[]{:S(2)}) collective-permute-start(f32[4,768]{1,0:T(4,128)S(1)} %get-tuple-element.27.refs_0_), channel_id=1, source_target_pairs={{0,2},{1,3},{2,0},{3,1},{4,6},{5,7},{6,4},{7,5},{8,10},{9,11},{10,... | collective-permute-start | bytes 36872 | tf_op jit(solution)/shard_map/ppermute | solution.py:489
  139.7 3.7 %collective-permute-start.6 = (f32[4,768]{1,0:T(4,128)S(1)}, f32[4,768]{1,0:T(4,128)S(1)}, u32[]{:S(2)}, u32[]{:S(2)}) collective-permute-start(f32[4,768]{1,0:T(4,128)S(1)} %get-tuple-element.27.refs_0_), channel_id=1, source_target_pairs={{0,1},{1,0},{2,3},{3,2},{4,5},{5,4},{6,7},{7,6},{8,9},{9,8},{10,11... | collective-permute-start | bytes 36872 | tf_op jit(solution)/shard_map/ppermute | solution.py:489
  143.5 1.2 collective-permute-start.9
  144.7 3.6 %collective-permute-start.10 = (f32[8,128]{1,0:T(8,128)S(1)}, f32[8,128]{1,0:T(8,128)S(1)}, u32[]{:S(2)}, u32[]{:S(2)}) collective-permute-start(f32[8,128]{1,0:T(8,128)S(1)} %add.9), channel_id=1, source_target_pairs={{0,8},{4,12},{8,0},{12,4},{16,24},{20,28},{24,16},{28,20},{1,9},{5... | collective-permute-start | bytes 12296 | tf_op jit(solution)/shard_map/ppermute | solution.py:489
  148.3 6.5 %collective-permute-start.11 = (f32[8,128]{1,0:T(8,128)S(1)}, f32[8,128]{1,0:T(8,128)S(1)}, u32[]{:S(2)}, u32[]{:S(2)}) collective-permute-start(f32[8,128]{1,0:T(8,128)S(1)} %add.10), channel_id=1, source_target_pairs={{0,16},{4,20},{8,24},{12,28},{16,0},{20,4},{24,8},{28,12},{1,17},{... | collective-permute-start | bytes 12296 | tf_op jit(solution)/shard_map/ppermute | solution.py:489
  149.8 5.0 %copy-start.2 = (f32[224,224]{1,0:T(8,128)S(1)}, f32[224,224]{1,0:T(8,128)}, u32[]{:S(2)}) copy-start(f32[224,224]{1,0:T(8,128)} %factor_ref.1) | copy-start | bytes 602116
  155.5 7.9 %collective-permute-start.14 = (f32[2,56,256]{2,1,0:T(8,128)S(1)}, f32[2,56,256]{2,1,0:T(8,128)S(1)}, u32[]{:S(2)}, u32[]{:S(2)}) collective-permute-start(f32[2,56,256]{2,1,0:T(8,128)S(1)} %get-tuple-element.34), channel_id=1, source_target_pairs={{0,3},{1,2},{2,1},{3,0},{4,7},{5,6},{6,5},{7,4},{8,11},{9,10},{10,... | collective-permute-start | bytes 344072 | tf_op jit(solution)/shard_map/ppermute | solution.py:489
  156.9 10.4 %collective-permute-start.13 = (f32[2,56,256]{2,1,0:T(8,128)S(1)}, f32[2,56,256]{2,1,0:T(8,128)S(1)}, u32[]{:S(2)}, u32[]{:S(2)}) collective-permute-start(f32[2,56,256]{2,1,0:T(8,128)S(1)} %get-tuple-element.35), channel_id=1, source_target_pairs={{0,2},{1,3},{2,0},{3,1},{4,6},{5,7},{6,4},{7,5},{8,10},{9,11},{10,... | collective-permute-start | bytes 344072 | tf_op jit(solution)/shard_map/ppermute | solution.py:489
  157.9 9.4 %collective-permute-start.12 = (f32[2,56,256]{2,1,0:T(8,128)S(1)}, f32[2,56,256]{2,1,0:T(8,128)S(1)}, u32[]{:S(2)}, u32[]{:S(2)}) collective-permute-start(f32[2,56,256]{2,1,0:T(8,128)S(1)} %get-tuple-element.36), channel_id=1, source_target_pairs={{0,1},{1,0},{2,3},{3,2},{4,5},{5,4},{6,7},{7,6},{8,9},{9,8},{10,11... | collective-permute-start | bytes 344072 | tf_op jit(solution)/shard_map/ppermute | solution.py:489
